TPU v7x, 256 devices: a whole 4x4x8 slice. The times are simulated.
256 devices in a mesh: dp: 4 (over x), gx: 16 (over y, z_lo, core), gy: 4 (over z_hi).
Axes of the slice: x: 4, y: 4, z: 8 (z_hi: 4, z_lo: 2; z = z_hi * 2 + z_lo), core: 2. Of those that a mesh axis runs over, the one named last changes fastest.
Arguments:
- field_in: bfloat16 [4, 32, 1024, 1024], P('dp', None, 'gx', 'gy'), parts along dimension 0, may hold values from -6 to 6
- spectral_weight: bfloat16 [32, 32, 2, 128, 128], P(None, None, None, ('gx', 'gy')), may hold values from -6 to 6
- conv_weight: bfloat16 [9, 32, 32], replicated, may hold values from -0.375 to 0.375
- conv_bias: float32 [32], replicated, may hold values from -3 to 3
- upstream: bfloat16 [4, 32, 1024, 1024], P('dp', None, 'gx', 'gy'), parts along dimension 0, may hold values from -6 to 6
Outputs:
- activation: float32 [4, 32, 1024, 1024], P('dp', None, 'gx', 'gy'), parts along dimension 0
- field_grad: float32 [4, 32, 1024, 1024], P('dp', None, 'gx', 'gy'), parts along dimension 0
- weight_grad: float32 [128, 32, 2, 128, 128], P('dp', None, None, ('gx', 'gy')), parts along dimension 0
There are 4 independent parts, one for each index of `dp`. A program takes and returns all parts, laid end to end along the dimension named above; an argument that names none is the same for every part. Nothing has to cross between parts.
All inputs are finite; a program needn't handle non-finite values.
Results may differ from a plain program's by a relative error of at most 0.02.
Values may be sent and summed in bfloat16 or wider, within the bound.
No kernel may reach another device: no remote copies, remote signals or barrier semaphores. Data moves between devices by JAX's collectives and lax.ppermute only.
A program may use at most 128 MiB of HBM per device.

v0:
```python
import math
import jax
import jax.numpy as jnp
from jax import lax
from jax.sharding import PartitionSpec as P

M1 = 128
M2 = 128


def padded_2(cells, sides, width):
    for axis, dim in sides:
        count = lax.axis_size(axis)
        ends = count - 1
        head = lax.slice_in_dim(cells, 0, width, axis=dim)
        tail = lax.slice_in_dim(cells, cells.shape[dim] - width, cells.shape[dim], axis=dim)
        cells = jnp.concatenate(
            [
                lax.ppermute(tail, axis, [(i, (i + 1) % count) for i in range(ends)]),
                cells,
                lax.ppermute(head, axis, [((i + 1) % count, i) for i in range(ends)]),
            ],
            axis=dim,
        )
    return cells


def kx_values(index, length, kept):
    return jnp.where(index < kept // 2, index, index + (length - kept))


def x_table(modes, positions, length):
    product = modes[:, None] * positions[None, :] % length
    angle = product.astype(jnp.float32) * (2.0 * math.pi / length)
    return jnp.stack([jnp.cos(angle), -jnp.sin(angle)], axis=1).astype(jnp.bfloat16)


def y_rows(length, kept, weighted):
    modes = jnp.arange(kept, dtype=jnp.int32)
    places = jnp.arange(length, dtype=jnp.int32)
    angle = (places[:, None] * modes[None, :] % length).astype(jnp.float32) * (
        2.0 * math.pi / length
    )
    cosine = jnp.cos(angle)
    sine = jnp.sin(angle)
    rows = jnp.stack(
        [jnp.stack([cosine, -sine], axis=1), jnp.stack([sine, cosine], axis=1)], axis=0
    )
    if weighted:
        rows = rows * jnp.where(modes == 0, 1.0, 2.0).astype(jnp.float32)
    return rows


def pdot(form, left, right):
    return jnp.einsum(form, left, right, preferred_element_type=jnp.float32)


def padded_block(field):
    return padded_2(field, (("gx", 2), ("gy", 3)), 1)


def forward_chain(field, ytab, factor):
    count_x = lax.axis_size("gx")
    strip_x = lax.axis_index("gx")
    width_x = field.shape[2]
    length_x = width_x * count_x
    positions = strip_x * width_x + jnp.arange(width_x, dtype=jnp.int32)
    modes = kx_values(
        jnp.arange(M1 // count_x * lax.axis_size("gx"), dtype=jnp.int32), length_x, M1
    )
    summed = lax.psum_scatter(
        pdot("msx,lcxy->mslcy", x_table(modes, positions, length_x), field),
        "gx",
        scatter_dimension=0,
        tiled=True,
    )
    spec_x = (summed * factor).astype(jnp.bfloat16)
    spec_x = lax.all_to_all(spec_x, "gy", split_axis=0, concat_axis=4, tiled=True)
    return pdot("mslcy,sytq->mtlcq", spec_x, ytab).astype(jnp.bfloat16)


def inverse_chain(spec, ytab, factor, width_x):
    count_x = lax.axis_size("gx")
    strip_x = lax.axis_index("gx")
    length_x = width_x * count_x
    over_y = pdot("mtldq,tqpy->mpldy", spec, ytab).astype(jnp.bfloat16)
    rows = lax.all_to_all(over_y, "gy", split_axis=4, concat_axis=0, tiled=True)
    positions = strip_x * width_x + jnp.arange(width_x, dtype=jnp.int32)
    piece = lax.all_gather(rows, "gx", axis=0, tiled=True)
    modes = kx_values(jnp.arange(piece.shape[0], dtype=jnp.int32), length_x, M1)
    total = pdot("mpldy,mpx->ldxy", piece, x_table(modes, positions, length_x))
    return (total * factor).astype(jnp.bfloat16)


def mix_modes(spec, weight):
    real_s, imag_s = (spec[:, 0], spec[:, 1])
    real_w, imag_w = (weight[:, :, 0], weight[:, :, 1])
    form = "mlcq,cdmq->mldq"
    real_v = pdot(form, real_s, real_w) - pdot(form, imag_s, imag_w)
    imag_v = pdot(form, real_s, imag_w) + pdot(form, imag_s, real_w)
    return jnp.stack([real_v, imag_v], axis=1).astype(jnp.bfloat16)


def mix_grads(spec, weight, dmixed):
    real_s, imag_s = (spec[:, 0], spec[:, 1])
    real_w, imag_w = (weight[:, :, 0], weight[:, :, 1])
    real_d, imag_d = (dmixed[:, 0], dmixed[:, 1])
    form_w = "mlcq,mldq->cdmq"
    grad_real = pdot(form_w, real_s, real_d) + pdot(form_w, imag_s, imag_d)
    grad_imag = pdot(form_w, real_s, imag_d) - pdot(form_w, imag_s, real_d)
    form_s = "cdmq,mldq->mlcq"
    dreal = pdot(form_s, real_w, real_d) + pdot(form_s, imag_w, imag_d)
    dimag = pdot(form_s, real_w, imag_d) - pdot(form_s, imag_w, real_d)
    grads = jnp.stack([grad_real, grad_imag], axis=2)
    return (grads, jnp.stack([dreal, dimag], axis=1).astype(jnp.bfloat16))


def conv_forward(padded, weight, rows, cols):
    total = jnp.zeros((padded.shape[0], weight.shape[1], rows, cols), jnp.float32)
    for row_tap in range(3):
        for col_tap in range(3):
            window = padded[:, :, row_tap : row_tap + rows, col_tap : col_tap + cols]
            total = total + pdot("dc,lcxy->ldxy", weight[3 * row_tap + col_tap], window)
    return total


def conv_backward(padded, weight, rows, cols):
    total = jnp.zeros((padded.shape[0], weight.shape[2], rows, cols), jnp.float32)
    for row_tap in range(3):
        for col_tap in range(3):
            window = padded[
                :, :, 2 - row_tap : 2 - row_tap + rows, 2 - col_tap : 2 - col_tap + cols
            ]
            total = total + pdot("dc,ldxy->lcxy", weight[3 * row_tap + col_tap], window)
    return total


def body(field_in, spectral_weight, conv_weight, conv_bias, upstream):
    width_x = field_in.shape[2]
    width_y = field_in.shape[3]
    length_y = width_y * lax.axis_size("gy")
    scale = 1.0 / (width_x * lax.axis_size("gx") * length_y)
    plain = y_rows(length_y, M2, False)
    weighted = y_rows(length_y, M2, True)
    fy_table = plain.astype(jnp.bfloat16)
    ay_table = weighted.astype(jnp.bfloat16)
    gy_table = jnp.transpose(weighted, (2, 3, 0, 1)).astype(jnp.bfloat16)
    by_table = jnp.transpose(plain, (2, 3, 0, 1)).astype(jnp.bfloat16)
    spec = forward_chain(field_in, fy_table, 1.0)
    mixed = mix_modes(spec, spectral_weight)
    spectral = inverse_chain(mixed, gy_table, scale, width_x)
    local = conv_forward(padded_block(field_in), conv_weight, width_x, width_y)
    pre = spectral.astype(jnp.float32) + local + conv_bias[None, :, None, None]
    gate = jax.nn.sigmoid(pre)
    activation = pre * gate
    dpre = (upstream.astype(jnp.float32) * gate * (1.0 + pre * (1.0 - gate))).astype(jnp.bfloat16)
    dspec = forward_chain(dpre, ay_table, scale)
    weight_grad, dmix = mix_grads(spec, spectral_weight, dspec)
    dfield = inverse_chain(dmix, by_table, 1.0, width_x)
    back_local = conv_backward(padded_block(dpre), conv_weight, width_x, width_y)
    field_grad = dfield.astype(jnp.float32) + back_local
    return (activation, field_grad, weight_grad)


def solution(mesh):
    return jax.shard_map(
        body,
        mesh=mesh,
        in_specs=(
            P("dp", None, "gx", "gy"),
            P(None, None, None, ("gx", "gy"), None),
            P(),
            P(),
            P("dp", None, "gx", "gy"),
        ),
        out_specs=(
            P("dp", None, "gx", "gy"),
            P("dp", None, "gx", "gy"),
            P("dp", None, None, ("gx", "gy"), None),
        ),
        check_vma=False,
    )
```

profile of v0, /device:TPU:33, one launch (start us, length us, event | category | flops | bytes accessed | tf_op | source)
XLA Modules:
  0.0 457.4 jit_solution(8955305337069914426)
XLA Ops:
  7.5 5.8 %convolution_bitcast_fusion.1 = f32[128,2,1,32,256]{4,0,3,1,2:T(8,128)} fusion(bf16[1,32,64,256]{3,2,1,0:T(8,128)(2,1)} %param.5, bf16[128,1,64]{0,2,1:T(8,128)(2,1)S(1)} %get-tuple-element.48, bf16[128,1,64]{0,2,1:T(8,128)(2,1)S(1)} %get-tuple-element.47), kind=kOutput, calls=%fused_computation.5 | convolution fusion | flops 268500992 | bytes 9469952 | tf_op jit(solution)/shard_map/msx,lcxy->mslcy/dot_general | solution.py:55
  13.2 1.9 fusion.106
  15.2 99.1 %reduce-scatter.3.cloned.1.call-done = f32[8,2,1,32,256]{4,0,3,1,2:T(8,128)} async-done(((f32[128,2,1,32,256]{4,0,3,1,2:T(8,128)}), f32[8,2,1,32,256]{4,0,3,1,2:T(8,128)}) %reduce-scatter.3.cloned.1.call-update) | async-done | bytes 524304 | tf_op jit(solution)/shard_map/reduce_scatter | solution.py:71
  116.1 6.7 %all-to-all-start = ((bf16[8,2,1,32,256]{4,3,1,2,0:T(8,128)(2,1)}), bf16[8,2,1,32,256]{4,3,1,2,0:T(8,128)(2,1)S(1)}, u32[]{:S(2)}, u32[]{:S(2)}) async-start(bf16[8,2,1,32,256]{4,3,1,2,0:T(8,128)(2,1)} %copy.63), calls=%async_computation.1 | async-start | bytes 524288 | tf_op jit(solution)/shard_map/all_to_all | solution.py:78
  122.9 2.1 fusion.104
  125.1 7.6 %all-to-all-done = bf16[8,2,1,32,256]{4,3,1,2,0:T(8,128)(2,1)S(1)} async-done(((bf16[8,2,1,32,256]{4,3,1,2,0:T(8,128)(2,1)}), bf16[8,2,1,32,256]{4,3,1,2,0:T(8,128)(2,1)S(1)}, u32[]{:S(2)}, u32[]{:S(2)}) %all-to-all-start) | async-done | bytes 262176 | tf_op jit(solution)/shard_map/all_to_all | solution.py:78
  135.8 2.1 fusion.26
  140.1 11.9 %all_to_all.66 = bf16[4,2,16384]{2,1,0:T(2,128)(2,1)S(1)} all-to-all(bf16[4,2,16384]{2,1,0:T(2,128)(2,1)S(1)} %reshape.513), channel_id=1, replica_groups=mesh['dp'=4,'gx'=16,'gy'=4] {'gy'}, dimensions={0} | all-to-all | bytes 524288 | tf_op jit(solution)/shard_map/all_to_all | solution.py:87
  152.5 1.4 copy.67
  155.4 5.6 %collective-permute-start = (bf16[1,32,1,256]{3,1,2,0:T(8,128)(2,1)S(1)}, bf16[1,32,1,256]{3,1,2,0:T(8,128)(2,1)S(1)}, u32[]{:S(2)}, u32[]{:S(2)}) collective-permute-start(bf16[1,32,1,256]{3,1,2,0:T(8,128)(2,1)S(1)} %get-tuple-element.34), channel_id=1, source_target_pairs={{0,4},{4,8},{8,12},{12,16},{16,20},{20,24},{24,28},{28,32},{32,36}... | collective-permute-start | bytes 49160 | tf_op jit(solution)/shard_map/ppermute | solution.py:19
  161.0 2.1 collective-permute-start.1
  163.2 2.1 fusion.92
  168.0 1.7 copy.76
  171.7 4.9 %collective-permute-start.2 = (bf16[1,32,66,1]{2,1,3,0:T(8,128)(2,1)S(1)}, bf16[1,32,66,1]{2,1,3,0:T(8,128)(2,1)S(1)}, u32[]{:S(2)}, u32[]{:S(2)}) collective-permute-start(bf16[1,32,66,1]{2,1,3,0:T(8,128)(2,1)S(1)} %copy.71), channel_id=1, source_target_pairs={{0,1},{1,2},{2,3},{4,5},{5,6},{6,7},{8,9},{9,10},{10,11},{12,13},{... | collective-permute-start | bytes 12680 | tf_op jit(solution)/shard_map/ppermute | solution.py:19
  176.6 1.7 fusion.57
  178.3 1.7 fusion.65
  181.9 2.0 fusion.36
  183.9 2.0 fusion.40
  185.9 1.9 fusion.44
  187.8 1.9 fusion.48
  189.6 1.9 fusion.61
  191.5 2.0 fusion.53
  193.5 9.3 %all-gather.3.cloned.1.call-done = bf16[128,2,1,32,256]{4,0,1,3,2:T(8,128)(2,1)} async-done(((bf16[8,2,1,32,256]{4,0,1,3,2:T(8,128)(2,1)}), bf16[128,2,1,32,256]{4,0,1,3,2:T(8,128)(2,1)}) %all-gather.3.cloned.1.call-update) | async-done | bytes 4194320 | tf_op jit(solution)/shard_map/all_gather | solution.py:89
  202.8 26.7 %multiply_convert_fusion = (bf16[1,32,64,256]{3,2,1,0:T(8,128)(2,1)S(1)}, f32[1,32,64,256]{3,2,1,0:T(8,128)}) fusion(bf16[1,32,64,256]{3,2,1,0:T(8,128)(2,1)S(1)} %copy-done.7, f32[32]{0:T(128)S(1)} %copy-done.12, f32[64,256,32]{1,2,0:T(8,128)} %fusion.53, f32[64,256,32]{1,2,0:T(8,128)} %fusion.57, f32[64,256,32]{1,2,0:T(8,128)} %fusion.61, ...), kind=kOutput, calls=%fused_computation.32 | convolution fusion | flops 281083904 | bytes 27295872 | tf_op jit(solution)/shard_map/mpldy,mpx->ldxy/dot_general | solution.py:55
  229.4 4.5 convolution_bitcast_fusion
  234.1 98.0 %reduce-scatter.5.cloned.1.call-done = f32[8,2,1,32,256]{4,0,3,1,2:T(8,128)} async-done(((f32[128,2,1,32,256]{4,0,3,1,2:T(8,128)}), f32[8,2,1,32,256]{4,0,3,1,2:T(8,128)}) %reduce-scatter.5.cloned.1.call-update) | async-done | bytes 524304 | tf_op jit(solution)/shard_map/reduce_scatter | solution.py:71
  333.2 17.9 %all_to_all.67 = bf16[8,2,1,32,256]{4,3,1,2,0:T(8,128)(2,1)S(1)} all-to-all(bf16[8,2,1,32,256]{4,3,1,2,0:T(8,128)(2,1)S(1)} %copy.87), channel_id=1, replica_groups=mesh['dp'=4,'gx'=16,'gy'=4] {'gy'}, dimensions={0} | all-to-all | bytes 524288 | tf_op jit(solution)/shard_map/all_to_all | solution.py:78
  354.2 2.6 fusion.30
  359.0 11.5 %all_to_all.68 = bf16[4,2,16384]{2,1,0:T(2,128)(2,1)S(1)} all-to-all(bf16[4,2,16384]{2,1,0:T(2,128)(2,1)S(1)} %reshape.515), channel_id=1, replica_groups=mesh['dp'=4,'gx'=16,'gy'=4] {'gy'}, dimensions={0} | all-to-all | bytes 524288 | tf_op jit(solution)/shard_map/all_to_all | solution.py:87
  371.1 1.4 copy.91
  373.4 5.0 %collective-permute-start.4 = (bf16[1,32,1,256]{3,2,1,0:T(2,128)(2,1)S(1)}, bf16[1,32,1,256]{3,2,1,0:T(2,128)(2,1)S(1)}, u32[]{:S(2)}, u32[]{:S(2)}) collective-permute-start(bf16[1,32,1,256]{3,2,1,0:T(2,128)(2,1)S(1)} %get-tuple-element.31), channel_id=1, source_target_pairs={{0,4},{4,8},{8,12},{12,16},{16,20},{20,24},{24,28},{28,32},{32,36}... | collective-permute-start | bytes 49160 | tf_op jit(solution)/shard_map/ppermute | solution.py:19
  378.5 1.9 collective-permute-start.5
  381.1 3.5 collective-permute-done.5
  386.6 1.4 copy.100
  388.0 3.8 collective-permute-start.7
  391.8 1.4 copy.92
  395.2 2.1 fusion.76
  397.3 2.1 fusion.88
  401.8 3.7 pad_maximum_fusion.2
  406.3 2.1 fusion.74
  408.4 2.2 slice_bitcast_fusion.5
  410.5 2.1 fusion.78
  412.7 2.1 fusion.80
  414.7 2.1 fusion.84
  416.8 2.1 fusion.86
  418.9 2.0 fusion.90
  422.2 2.4 pad_maximum_fusion.1
  424.6 25.9 %bitcast_add_fusion = f32[1,32,64,256]{3,2,1,0:T(8,128)} fusion(f32[64,256,32]{1,2,0:T(8,128)} %fusion.74, f32[64,256,32]{1,2,0:T(8,128)} %fusion.76, f32[64,256,32]{1,2,0:T(8,128)} %fusion.78, f32[64,256,32]{1,2,0:T(8,128)} %fusion.80, f32[64,256,32]{1,2,0:T(8,128)S(1)} %fusion.82, f32[64,256,32]{1,2,0:T(8,128)} %fusion.84, f32[64,256,32]{1,2,0:T(8,128)} %fusion.86, ...), kind=kOutput, calls=%fused_computation.8 | convolution fusion | flops 274268160 | bytes 25198592 | tf_op jit(solution)/shard_map/mpldy,mpx->ldxy/dot_general | solution.py:55
  (101 shorter events, 33.1 us)
Async XLA Ops:
  7.2 107.1 %reduce-scatter.3.cloned.1.call-start = ((), (), s32[]{:S(2)}) async-start(), calls=%async_computation.6 | async-start | bytes 8912896 | tf_op jit(solution)/shard_map/reduce_scatter | solution.py:71
  116.1 16.6 %all-to-all-start = ((bf16[8,2,1,32,256]{4,3,1,2,0:T(8,128)(2,1)}), bf16[8,2,1,32,256]{4,3,1,2,0:T(8,128)(2,1)S(1)}, u32[]{:S(2)}, u32[]{:S(2)}) async-start(bf16[8,2,1,32,256]{4,3,1,2,0:T(8,128)(2,1)} %copy.63), calls=%async_computation.1 | async-start | bytes 524288 | tf_op jit(solution)/shard_map/all_to_all | solution.py:78
  122.9 79.9 %all-gather.3.cloned.1.call-start = ((), (), s32[]{:S(2)}) async-start(), calls=%async_computation.7 | async-start | bytes 4456448 | tf_op jit(solution)/shard_map/all_gather | solution.py:89
  125.1 12.8 %copy-start.1 = (f32[1,1024,2,128]{3,1,0,2:T(8,128)}, f32[1,1024,2,128]{3,1,0,2:T(8,128)S(1)}, u32[]{:S(2)}) copy-start(f32[1,1024,2,128]{3,1,0,2:T(8,128)S(1)} %get-tuple-element.35) | copy-start | bytes 3145732
  125.1 12.8 %copy-start.3 = (f32[1,1024,2,128]{3,1,0,2:T(8,128)}, f32[1,1024,2,128]{3,1,0,2:T(8,128)S(1)}, u32[]{:S(2)}) copy-start(f32[1,1024,2,128]{3,1,0,2:T(8,128)S(1)} %get-tuple-element.36) | copy-start | bytes 3145732
  125.1 10.7 %copy-start.5 = (bf16[32,32,2,2,128]{4,3,2,1,0:T(2,128)(2,1)S(1)}, bf16[32,32,2,2,128]{4,3,2,1,0:T(2,128)(2,1)}, u32[]{:S(2)}) copy-start(bf16[32,32,2,2,128]{4,3,2,1,0:T(2,128)(2,1)} %param.6) | copy-start | bytes 3145732
  140.1 14.7 %copy-start = (bf16[1,32,64,256]{3,2,1,0:T(8,128)(2,1)S(1)}, bf16[1,32,64,256]{3,2,1,0:T(8,128)(2,1)}, u32[]{:S(2)}) copy-start(bf16[1,32,64,256]{3,2,1,0:T(8,128)(2,1)} %param.5) | copy-start | bytes 3145732
  152.5 10.7 %copy-start.8 = (bf16[9,32,32]{2,1,0:T(8,128)(2,1)S(1)}, bf16[9,32,32]{2,1,0:T(8,128)(2,1)}, u32[]{:S(2)}) copy-start(bf16[9,32,32]{2,1,0:T(8,128)(2,1)} %param.7) | copy-start | bytes 55300
  154.7 177.3 %reduce-scatter.5.cloned.1.call-start = ((), (), s32[]{:S(2)}) async-start(), calls=%async_computation.8 | async-start | bytes 8912896 | tf_op jit(solution)/shard_map/reduce_scatter | solution.py:71
  155.4 9.9 %collective-permute-start = (bf16[1,32,1,256]{3,1,2,0:T(8,128)(2,1)S(1)}, bf16[1,32,1,256]{3,1,2,0:T(8,128)(2,1)S(1)}, u32[]{:S(2)}, u32[]{:S(2)}) collective-permute-start(bf16[1,32,1,256]{3,1,2,0:T(8,128)(2,1)S(1)} %get-tuple-element.34), channel_id=1, source_target_pairs={{0,4},{4,8},{8,12},{12,16},{16,20},{20,24},{24,28},{28,32},{32,36}... | collective-permute-start | bytes 49160 | tf_op jit(solution)/shard_map/ppermute | solution.py:19
  161.0 6.0 %collective-permute-start.1 = (bf16[1,32,1,256]{3,1,2,0:T(8,128)(2,1)S(1)}, bf16[1,32,1,256]{3,1,2,0:T(8,128)(2,1)S(1)}, u32[]{:S(2)}, u32[]{:S(2)}) collective-permute-start(bf16[1,32,1,256]{3,1,2,0:T(8,128)(2,1)S(1)} %get-tuple-element.33), channel_id=1, source_target_pairs={{4,0},{8,4},{12,8},{16,12},{20,16},{24,20},{28,24},{32,28},{36,32}... | collective-permute-start | bytes 49160 | tf_op jit(solution)/shard_map/ppermute | solution.py:21
  169.7 10.3 %collective-permute-start.3 = (bf16[1,32,66,1]{2,1,3,0:T(8,128)(2,1)S(1)}, bf16[1,32,66,1]{2,1,3,0:T(8,128)(2,1)S(1)}, u32[]{:S(2)}, u32[]{:S(2)}) collective-permute-start(bf16[1,32,66,1]{2,1,3,0:T(8,128)(2,1)S(1)} %copy.76), channel_id=1, source_target_pairs={{1,0},{2,1},{3,2},{5,4},{6,5},{7,6},{9,8},{10,9},{11,10},{13,12},{... | collective-permute-start | bytes 12680 | tf_op jit(solution)/shard_map/ppermute | solution.py:21
  171.7 9.3 %collective-permute-start.2 = (bf16[1,32,66,1]{2,1,3,0:T(8,128)(2,1)S(1)}, bf16[1,32,66,1]{2,1,3,0:T(8,128)(2,1)S(1)}, u32[]{:S(2)}, u32[]{:S(2)}) collective-permute-start(bf16[1,32,66,1]{2,1,3,0:T(8,128)(2,1)S(1)} %copy.71), channel_id=1, source_target_pairs={{0,1},{1,2},{2,3},{4,5},{5,6},{6,7},{8,9},{9,10},{10,11},{12,13},{... | collective-permute-start | bytes 12680 | tf_op jit(solution)/shard_map/ppermute | solution.py:19
  191.5 11.2 %copy-start.7 = (bf16[1,32,64,256]{3,2,1,0:T(8,128)(2,1)S(1)}, bf16[1,32,64,256]{3,2,1,0:T(8,128)(2,1)}, u32[]{:S(2)}) copy-start(bf16[1,32,64,256]{3,2,1,0:T(8,128)(2,1)} %param.9) | copy-start | bytes 3145732
  191.5 11.2 %copy-start.12 = (f32[32]{0:T(128)S(1)}, f32[32]{0:T(128)}, u32[]{:S(2)}) copy-start(f32[32]{0:T(128)} %param.8) | copy-start | bytes 388
  234.0 118.2 %copy-start.2 = (f32[1,1024,2,128]{3,1,0,2:T(8,128)S(1)}, f32[1,1024,2,128]{3,1,0,2:T(8,128)}, u32[]{:S(2)}) copy-start(f32[1,1024,2,128]{3,1,0,2:T(8,128)} %copy-done.1) | copy-start | bytes 3145732
  234.0 118.2 %copy-start.4 = (f32[1,1024,2,128]{3,1,0,2:T(8,128)S(1)}, f32[1,1024,2,128]{3,1,0,2:T(8,128)}, u32[]{:S(2)}) copy-start(f32[1,1024,2,128]{3,1,0,2:T(8,128)} %copy-done.3) | copy-start | bytes 3145732
  234.0 190.6 %all-gather.5.cloned.1.call-start = ((), (), s32[]{:S(2)}) async-start(), calls=%async_computation.9 | async-start | bytes 4456448 | tf_op jit(solution)/shard_map/all_gather | solution.py:89
  352.2 2.0 copy-start.6
  359.0 14.3 %copy-start.9 = (f32[2,128,32]{1,2,0:T(8,128)S(1)}, f32[2,128,32]{1,2,0:T(8,128)}, u32[]{:S(2)}) copy-start(f32[2,128,32]{1,2,0:T(8,128)} %get-tuple-element.43) | copy-start | bytes 98308
  373.4 7.7 %collective-permute-start.4 = (bf16[1,32,1,256]{3,2,1,0:T(2,128)(2,1)S(1)}, bf16[1,32,1,256]{3,2,1,0:T(2,128)(2,1)S(1)}, u32[]{:S(2)}, u32[]{:S(2)}) collective-permute-start(bf16[1,32,1,256]{3,2,1,0:T(2,128)(2,1)S(1)} %get-tuple-element.31), channel_id=1, source_target_pairs={{0,4},{4,8},{8,12},{12,16},{16,20},{20,24},{24,28},{28,32},{32,36}... | collective-permute-start | bytes 49160 | tf_op jit(solution)/shard_map/ppermute | solution.py:19
  378.5 6.1 %collective-permute-start.5 = (bf16[1,32,1,256]{3,2,1,0:T(2,128)(2,1)S(1)}, bf16[1,32,1,256]{3,2,1,0:T(2,128)(2,1)S(1)}, u32[]{:S(2)}, u32[]{:S(2)}) collective-permute-start(bf16[1,32,1,256]{3,2,1,0:T(2,128)(2,1)S(1)} %get-tuple-element.32), channel_id=1, source_target_pairs={{4,0},{8,4},{12,8},{16,12},{20,16},{24,20},{28,24},{32,28},{36,32}... | collective-permute-start | bytes 49160 | tf_op jit(solution)/shard_map/ppermute | solution.py:21
  388.0 11.5 %collective-permute-start.7 = (bf16[1,32,66,1]{2,1,3,0:T(8,128)(2,1)S(1)}, bf16[1,32,66,1]{2,1,3,0:T(8,128)(2,1)S(1)}, u32[]{:S(2)}, u32[]{:S(2)}) collective-permute-start(bf16[1,32,66,1]{2,1,3,0:T(8,128)(2,1)S(1)} %copy.100), channel_id=1, source_target_pairs={{0,1},{1,2},{2,3},{4,5},{5,6},{6,7},{8,9},{9,10},{10,11},{12,13},{... | collective-permute-start | bytes 12680 | tf_op jit(solution)/shard_map/ppermute | solution.py:19
  393.2 7.4 %collective-permute-start.6 = (bf16[1,32,66,1]{2,1,3,0:T(8,128)(2,1)S(1)}, bf16[1,32,66,1]{2,1,3,0:T(8,128)(2,1)S(1)}, u32[]{:S(2)}, u32[]{:S(2)}) collective-permute-start(bf16[1,32,66,1]{2,1,3,0:T(8,128)(2,1)S(1)} %copy.92), channel_id=1, source_target_pairs={{1,0},{2,1},{3,2},{5,4},{6,5},{7,6},{9,8},{10,9},{11,10},{13,12},{... | collective-permute-start | bytes 12680 | tf_op jit(solution)/shard_map/ppermute | solution.py:21
  418.9 2.1 copy-start.11
  418.9 2.1 copy-start.10
Sparse Core Ops, SparseCore 0:
  13.4 100.8 reduce-scatter.2
  154.8 47.8 all-gather.2
  234.1 97.9 reduce-scatter.4
  373.4 46.9 all-gather.4
where the time goes:
time: 466 us; the launch traced here: 457 us
  waiting for transfers between devices  219 us (47%)
  matrix products  99.8 us (21%)
  blocking collectives  41.3 us (9%)
  starting transfers between devices  32.9 us (7%)
  local copies, waits for them, and re-layouts  28.8 us (6%)
  other arithmetic  21.3 us (5%)
  between operations  14.7 us (3%)
    reduce_scatter x2, waiting for transfers between devices, forward_chain(): lax.psum_scatter(pdot('msx,lcxy->mslcy', x_table(modes, positions, length...  197 us
    dot_general x26, matrix products, pdot(): return jnp.einsum(form, left, right, preferred_element_type=jnp.float32)  99.8 us
    all_to_all x2, blocking collectives, inverse_chain(): rows = lax.all_to_all(over_y, 'gy', split_axis=4, concat_axis=0, tiled=True)  23.4 us
    ppermute x4, starting transfers between devices, padded_2(): lax.ppermute(tail, axis, [(i, (i + 1) % count) for i in range(ends)])  19.4 us
    all_to_all x1, blocking collectives, forward_chain(): lax.all_to_all(spec_x, 'gy', split_axis=0, concat_axis=4, tiled=True)  17.9 us
  transfers between devices with their start and end apart: 13, of which 6 were waited for; matrix products, arithmetic and copies ran while one was open for 14% of the time, Pallas kernels for 0%

commit v1 on v0

--- a/solution.py
+++ b/solution.py
@@ -86,7 +86,9 @@
     over_y = pdot("mtldq,tqpy->mpldy", spec, ytab).astype(jnp.bfloat16)
     rows = lax.all_to_all(over_y, "gy", split_axis=4, concat_axis=0, tiled=True)
     positions = strip_x * width_x + jnp.arange(width_x, dtype=jnp.int32)
-    piece = lax.all_gather(rows, "gx", axis=0, tiled=True)
+    piece = jnp.concatenate(
+        lax.all_to_all(jnp.stack([rows] * lax.axis_size("gx")), "gx", 0, 0), axis=0
+    )
     modes = kx_values(jnp.arange(piece.shape[0], dtype=jnp.int32), length_x, M1)
     total = pdot("mpldy,mpx->ldxy", piece, x_table(modes, positions, length_x))
     return (total * factor).astype(jnp.bfloat16)

time: 466 us -> 552 us (1.18)
  the two profiles are of different devices: /device:TPU:33 before, /device:TPU:1 now
where the time goes in v1:
time: 552 us; the launch traced here: 543 us
  waiting for transfers between devices  289 us (52%)
  matrix products  99.8 us (18%)
  starting transfers between devices  47.2 us (9%)
  blocking collectives  39.3 us (7%)
  local copies, waits for them, and re-layouts  30.7 us (6%)
  other arithmetic  21.2 us (4%)
  between operations  15 us (3%)
    reduce_scatter x2, waiting for transfers between devices, forward_chain(): lax.psum_scatter(pdot('msx,lcxy->mslcy', x_table(modes, positions, length...  198 us
    dot_general x26, matrix products, pdot(): return jnp.einsum(form, left, right, preferred_element_type=jnp.float32)  99.8 us
    ppermute x4, waiting for transfers between devices, padded_2(): lax.ppermute(tail, axis, [(i, (i + 1) % count) for i in range(ends)])  79.7 us
    all_to_all x2, blocking collectives, inverse_chain(): rows = lax.all_to_all(over_y, 'gy', split_axis=4, concat_axis=0, tiled=True)  23.8 us
    all_to_all x2, starting transfers between devices, inverse_chain(): lax.all_to_all(jnp.stack([rows] * lax.axis_size('gx')), 'gx', 0, 0)  17.9 us
    ppermute x4, starting transfers between devices, padded_2(): lax.ppermute(tail, axis, [(i, (i + 1) % count) for i in range(ends)])  16.8 us
    all_to_all x1, blocking collectives, forward_chain(): lax.all_to_all(spec_x, 'gy', split_axis=0, concat_axis=4, tiled=True)  15.5 us
  transfers between devices with their start and end apart: 13, of which 7 were waited for; matrix products, arithmetic and copies ran while one was open for 11% of the time, Pallas kernels for 0%

profile of v1, /device:TPU:1, one launch (start us, length us, event | category | flops | bytes accessed | tf_op | source)
XLA Modules:
  0.0 542.5 jit_solution(702526747833545362)
XLA Ops:
  7.5 5.7 %convolution_bitcast_fusion.1 = f32[128,2,1,32,256]{4,0,3,1,2:T(8,128)} fusion(bf16[1,32,64,256]{3,2,1,0:T(8,128)(2,1)} %param.5, bf16[128,1,64]{0,2,1:T(8,128)(2,1)S(1)} %get-tuple-element.48, bf16[128,1,64]{0,2,1:T(8,128)(2,1)S(1)} %get-tuple-element.47), kind=kOutput, calls=%fused_computation.7 | convolution fusion | flops 268500992 | bytes 9469952 | tf_op jit(solution)/shard_map/msx,lcxy->mslcy/dot_general | solution.py:55
  13.2 1.9 fusion.108
  15.2 100.7 %reduce-scatter.3.cloned.1.call-done = f32[8,2,1,32,256]{4,0,3,1,2:T(8,128)} async-done(((f32[128,2,1,32,256]{4,0,3,1,2:T(8,128)}), f32[8,2,1,32,256]{4,0,3,1,2:T(8,128)}) %reduce-scatter.3.cloned.1.call-update) | async-done | bytes 524304 | tf_op jit(solution)/shard_map/reduce_scatter | solution.py:71
  117.7 5.8 %all-to-all-start = ((bf16[8,2,1,32,256]{4,3,1,2,0:T(8,128)(2,1)}), bf16[8,2,1,32,256]{4,3,1,2,0:T(8,128)(2,1)S(1)}, u32[]{:S(2)}, u32[]{:S(2)}) async-start(bf16[8,2,1,32,256]{4,3,1,2,0:T(8,128)(2,1)} %copy.185), calls=%async_computation.1 | async-start | bytes 524288 | tf_op jit(solution)/shard_map/all_to_all | solution.py:78
  123.6 2.1 fusion.106
  125.8 7.2 %all-to-all-done = bf16[8,2,1,32,256]{4,3,1,2,0:T(8,128)(2,1)S(1)} async-done(((bf16[8,2,1,32,256]{4,3,1,2,0:T(8,128)(2,1)}), bf16[8,2,1,32,256]{4,3,1,2,0:T(8,128)(2,1)S(1)}, u32[]{:S(2)}, u32[]{:S(2)}) %all-to-all-start) | async-done | bytes 262176 | tf_op jit(solution)/shard_map/all_to_all | solution.py:78
  136.1 2.1 fusion.28
  140.3 11.8 %all_to_all.70 = bf16[4,2,16384]{2,1,0:T(2,128)(2,1)S(1)} all-to-all(bf16[4,2,16384]{2,1,0:T(2,128)(2,1)S(1)} %reshape.527), channel_id=1, replica_groups=mesh['dp'=4,'gx'=16,'gy'=4] {'gy'}, dimensions={0} | all-to-all | bytes 524288 | tf_op jit(solution)/shard_map/all_to_all | solution.py:87
  154.3 2.4 stack.39
  156.7 9.0 %all-to-all-start.2 = ((bf16[16,8,2,1,32,256]{5,1,2,4,3,0:T(8,128)(2,1)}), bf16[16,8,2,1,32,256]{5,1,2,4,3,0:T(8,128)(2,1)}, u32[]{:S(2)}, u32[]{:S(2)}) async-start(bf16[16,8,2,1,32,256]{5,1,2,4,3,0:T(8,128)(2,1)} %stack.39), calls=%async_computation.3 | async-start | bytes 8388608 | tf_op jit(solution)/shard_map/all_to_all | solution.py:90
  166.3 3.5 collective-permute-start
  169.9 2.1 collective-permute-start.1
  172.0 2.1 fusion.94
  174.1 38.6 %collective-permute-done = bf16[1,32,1,256]{3,1,2,0:T(8,128)(2,1)S(1)} collective-permute-done((bf16[1,32,1,256]{3,1,2,0:T(8,128)(2,1)S(1)}, bf16[1,32,1,256]{3,1,2,0:T(8,128)(2,1)S(1)}, u32[]{:S(2)}, u32[]{:S(2)}) %collective-permute-start) | collective-permute-done | bytes 16416 | tf_op jit(solution)/shard_map/ppermute | solution.py:19
  213.3 1.8 collective-permute-done.1
  218.0 4.9 collective-permute-start.2
  222.9 1.7 fusion.59
  228.3 2.0 fusion.38
  230.3 2.0 fusion.42
  232.2 1.8 fusion.46
  234.1 1.9 fusion.50
  236.0 1.9 fusion.63
  237.9 2.0 fusion.55
  239.9 26.5 %multiply_convert_fusion = (bf16[1,32,64,256]{3,2,1,0:T(8,128)(2,1)S(1)}, f32[1,32,64,256]{3,2,1,0:T(8,128)}) fusion(bf16[1,32,64,256]{3,2,1,0:T(8,128)(2,1)S(1)} %copy-done.7, f32[32]{0:T(128)S(1)} %copy-done.12, f32[64,256,32]{1,2,0:T(8,128)} %fusion.55, f32[64,256,32]{1,2,0:T(8,128)} %fusion.59, f32[64,256,32]{1,2,0:T(8,128)} %fusion.63, ...), kind=kOutput, calls=%fused_computation.34 | convolution fusion | flops 281083904 | bytes 27295872 | tf_op jit(solution)/shard_map/mpldy,mpx->ldxy/dot_general | solution.py:55
  266.4 4.5 convolution_bitcast_fusion
  271.0 97.5 %reduce-scatter.5.cloned.1.call-done = f32[8,2,1,32,256]{4,0,3,1,2:T(8,128)} async-done(((f32[128,2,1,32,256]{4,0,3,1,2:T(8,128)}), f32[8,2,1,32,256]{4,0,3,1,2:T(8,128)}) %reduce-scatter.5.cloned.1.call-update) | async-done | bytes 524304 | tf_op jit(solution)/shard_map/reduce_scatter | solution.py:71
  369.6 15.5 %all_to_all.71 = bf16[8,2,1,32,256]{4,3,1,2,0:T(8,128)(2,1)S(1)} all-to-all(bf16[8,2,1,32,256]{4,3,1,2,0:T(8,128)(2,1)S(1)} %copy.212), channel_id=1, replica_groups=mesh['dp'=4,'gx'=16,'gy'=4] {'gy'}, dimensions={0} | all-to-all | bytes 524288 | tf_op jit(solution)/shard_map/all_to_all | solution.py:78
  388.3 2.6 fusion.32
  393.0 12.0 %all_to_all.72 = bf16[4,2,16384]{2,1,0:T(2,128)(2,1)S(1)} all-to-all(bf16[4,2,16384]{2,1,0:T(2,128)(2,1)S(1)} %reshape.529), channel_id=1, replica_groups=mesh['dp'=4,'gx'=16,'gy'=4] {'gy'}, dimensions={0} | all-to-all | bytes 524288 | tf_op jit(solution)/shard_map/all_to_all | solution.py:87
  407.2 2.4 stack.42
  409.6 8.8 %all-to-all-start.5 = ((bf16[16,8,2,1,32,256]{5,1,2,4,3,0:T(8,128)(2,1)}), bf16[16,8,2,1,32,256]{5,1,2,4,3,0:T(8,128)(2,1)}, u32[]{:S(2)}, u32[]{:S(2)}) async-start(bf16[16,8,2,1,32,256]{5,1,2,4,3,0:T(8,128)(2,1)} %stack.42), calls=%async_computation.7 | async-start | bytes 8388608 | tf_op jit(solution)/shard_map/all_to_all | solution.py:90
  418.6 3.5 collective-permute-start.4
  422.1 1.9 collective-permute-start.5
  424.8 41.1 %collective-permute-done.4 = bf16[1,32,1,256]{3,2,1,0:T(2,128)(2,1)S(1)} collective-permute-done((bf16[1,32,1,256]{3,2,1,0:T(2,128)(2,1)S(1)}, bf16[1,32,1,256]{3,2,1,0:T(2,128)(2,1)S(1)}, u32[]{:S(2)}, u32[]{:S(2)}) %collective-permute-start.4) | collective-permute-done | bytes 16416 | tf_op jit(solution)/shard_map/ppermute | solution.py:19
  465.9 2.4 collective-permute-done.5
  474.3 4.9 collective-permute-start.7
  479.9 2.1 fusion.78
  482.0 2.1 fusion.90
  486.5 3.7 pad_maximum_fusion.2
  490.9 2.1 fusion.76
  493.1 2.2 slice_bitcast_fusion.5
  495.3 2.1 fusion.80
  497.3 2.0 fusion.82
  499.4 2.1 fusion.86
  501.5 2.1 fusion.88
  503.5 2.1 fusion.92
  506.9 2.4 pad_maximum_fusion.1
  509.3 25.9 %bitcast_add_fusion = f32[1,32,64,256]{3,2,1,0:T(8,128)} fusion(f32[64,256,32]{1,2,0:T(8,128)} %fusion.76, f32[64,256,32]{1,2,0:T(8,128)} %fusion.78, f32[64,256,32]{1,2,0:T(8,128)} %fusion.80, f32[64,256,32]{1,2,0:T(8,128)} %fusion.82, f32[64,256,32]{1,2,0:T(8,128)S(1)} %fusion.84, f32[64,256,32]{1,2,0:T(8,128)} %fusion.86, f32[64,256,32]{1,2,0:T(8,128)} %fusion.88, ...), kind=kOutput, calls=%fused_computation.10 | convolution fusion | flops 274268160 | bytes 25198592 | tf_op jit(solution)/shard_map/mpldy,mpx->ldxy/dot_general | solution.py:55
  (103 shorter events, 37.9 us)
Async XLA Ops:
  7.2 108.7 %reduce-scatter.3.cloned.1.call-start = ((), (), s32[]{:S(2)}) async-start(), calls=%async_computation.8 | async-start | bytes 8912896 | tf_op jit(solution)/shard_map/reduce_scatter | solution.py:71
  117.7 15.3 %all-to-all-start = ((bf16[8,2,1,32,256]{4,3,1,2,0:T(8,128)(2,1)}), bf16[8,2,1,32,256]{4,3,1,2,0:T(8,128)(2,1)S(1)}, u32[]{:S(2)}, u32[]{:S(2)}) async-start(bf16[8,2,1,32,256]{4,3,1,2,0:T(8,128)(2,1)} %copy.185), calls=%async_computation.1 | async-start | bytes 524288 | tf_op jit(solution)/shard_map/all_to_all | solution.py:78
  125.8 12.3 %copy-start.1 = (f32[1,1024,2,128]{3,1,0,2:T(8,128)}, f32[1,1024,2,128]{3,1,0,2:T(8,128)S(1)}, u32[]{:S(2)}) copy-start(f32[1,1024,2,128]{3,1,0,2:T(8,128)S(1)} %get-tuple-element.35) | copy-start | bytes 3145732
  125.8 12.3 %copy-start.3 = (f32[1,1024,2,128]{3,1,0,2:T(8,128)}, f32[1,1024,2,128]{3,1,0,2:T(8,128)S(1)}, u32[]{:S(2)}) copy-start(f32[1,1024,2,128]{3,1,0,2:T(8,128)S(1)} %get-tuple-element.36) | copy-start | bytes 3145732
  125.8 10.2 %copy-start.5 = (bf16[32,32,2,2,128]{4,3,2,1,0:T(2,128)(2,1)S(1)}, bf16[32,32,2,2,128]{4,3,2,1,0:T(2,128)(2,1)}, u32[]{:S(2)}) copy-start(bf16[32,32,2,2,128]{4,3,2,1,0:T(2,128)(2,1)} %param.6) | copy-start | bytes 3145732
  156.7 9.1 %copy-start = (bf16[1,32,64,256]{3,2,1,0:T(8,128)(2,1)S(1)}, bf16[1,32,64,256]{3,2,1,0:T(8,128)(2,1)}, u32[]{:S(2)}) copy-start(bf16[1,32,64,256]{3,2,1,0:T(8,128)(2,1)} %param.5) | copy-start | bytes 3145732
  156.7 83.2 %all-to-all-start.2 = ((bf16[16,8,2,1,32,256]{5,1,2,4,3,0:T(8,128)(2,1)}), bf16[16,8,2,1,32,256]{5,1,2,4,3,0:T(8,128)(2,1)}, u32[]{:S(2)}, u32[]{:S(2)}) async-start(bf16[16,8,2,1,32,256]{5,1,2,4,3,0:T(8,128)(2,1)} %stack.39), calls=%async_computation.3 | async-start | bytes 8388608 | tf_op jit(solution)/shard_map/all_to_all | solution.py:90
  165.7 6.4 %copy-start.8 = (bf16[9,32,32]{2,1,0:T(8,128)(2,1)S(1)}, bf16[9,32,32]{2,1,0:T(8,128)(2,1)}, u32[]{:S(2)}) copy-start(bf16[9,32,32]{2,1,0:T(8,128)(2,1)} %param.7) | copy-start | bytes 55300
  165.7 202.8 %reduce-scatter.5.cloned.1.call-start = ((), (), s32[]{:S(2)}) async-start(), calls=%async_computation.9 | async-start | bytes 8912896 | tf_op jit(solution)/shard_map/reduce_scatter | solution.py:71
  166.3 46.4 %collective-permute-start = (bf16[1,32,1,256]{3,1,2,0:T(8,128)(2,1)S(1)}, bf16[1,32,1,256]{3,1,2,0:T(8,128)(2,1)S(1)}, u32[]{:S(2)}, u32[]{:S(2)}) collective-permute-start(bf16[1,32,1,256]{3,1,2,0:T(8,128)(2,1)S(1)} %get-tuple-element.34), channel_id=1, source_target_pairs={{0,4},{4,8},{8,12},{12,16},{16,20},{20,24},{24,28},{28,32},{32,36}... | collective-permute-start | bytes 49160 | tf_op jit(solution)/shard_map/ppermute | solution.py:19
  169.9 45.2 %collective-permute-start.1 = (bf16[1,32,1,256]{3,1,2,0:T(8,128)(2,1)S(1)}, bf16[1,32,1,256]{3,1,2,0:T(8,128)(2,1)S(1)}, u32[]{:S(2)}, u32[]{:S(2)}) collective-permute-start(bf16[1,32,1,256]{3,1,2,0:T(8,128)(2,1)S(1)} %get-tuple-element.33), channel_id=1, source_target_pairs={{4,0},{8,4},{12,8},{16,12},{20,16},{24,20},{28,24},{32,28},{36,32}... | collective-permute-start | bytes 49160 | tf_op jit(solution)/shard_map/ppermute | solution.py:21
  216.1 10.3 %collective-permute-start.3 = (bf16[1,32,66,1]{2,1,3,0:T(8,128)(2,1)S(1)}, bf16[1,32,66,1]{2,1,3,0:T(8,128)(2,1)S(1)}, u32[]{:S(2)}, u32[]{:S(2)}) collective-permute-start(bf16[1,32,66,1]{2,1,3,0:T(8,128)(2,1)S(1)} %copy.201), channel_id=1, source_target_pairs={{1,0},{2,1},{3,2},{5,4},{6,5},{7,6},{9,8},{10,9},{11,10},{13,12},{... | collective-permute-start | bytes 12680 | tf_op jit(solution)/shard_map/ppermute | solution.py:21
  218.0 9.3 %collective-permute-start.2 = (bf16[1,32,66,1]{2,1,3,0:T(8,128)(2,1)S(1)}, bf16[1,32,66,1]{2,1,3,0:T(8,128)(2,1)S(1)}, u32[]{:S(2)}, u32[]{:S(2)}) collective-permute-start(bf16[1,32,66,1]{2,1,3,0:T(8,128)(2,1)S(1)} %copy.196), channel_id=1, source_target_pairs={{0,1},{1,2},{2,3},{4,5},{5,6},{6,7},{8,9},{9,10},{10,11},{12,13},{... | collective-permute-start | bytes 12680 | tf_op jit(solution)/shard_map/ppermute | solution.py:19
  237.9 2.0 copy-start.7
  237.9 2.0 copy-start.12
  271.0 115.2 %copy-start.2 = (f32[1,1024,2,128]{3,1,0,2:T(8,128)S(1)}, f32[1,1024,2,128]{3,1,0,2:T(8,128)}, u32[]{:S(2)}) copy-start(f32[1,1024,2,128]{3,1,0,2:T(8,128)} %copy-done.1) | copy-start | bytes 3145732
  271.0 115.2 %copy-start.4 = (f32[1,1024,2,128]{3,1,0,2:T(8,128)S(1)}, f32[1,1024,2,128]{3,1,0,2:T(8,128)}, u32[]{:S(2)}) copy-start(f32[1,1024,2,128]{3,1,0,2:T(8,128)} %copy-done.3) | copy-start | bytes 3145732
  386.2 2.0 copy-start.6
  409.6 8.9 %copy-start.9 = (f32[2,128,32]{1,2,0:T(8,128)S(1)}, f32[2,128,32]{1,2,0:T(8,128)}, u32[]{:S(2)}) copy-start(f32[2,128,32]{1,2,0:T(8,128)} %get-tuple-element.43) | copy-start | bytes 98308
  409.6 99.7 %all-to-all-start.5 = ((bf16[16,8,2,1,32,256]{5,1,2,4,3,0:T(8,128)(2,1)}), bf16[16,8,2,1,32,256]{5,1,2,4,3,0:T(8,128)(2,1)}, u32[]{:S(2)}, u32[]{:S(2)}) async-start(bf16[16,8,2,1,32,256]{5,1,2,4,3,0:T(8,128)(2,1)} %stack.42), calls=%async_computation.7 | async-start | bytes 8388608 | tf_op jit(solution)/shard_map/all_to_all | solution.py:90
  418.6 47.3 %collective-permute-start.4 = (bf16[1,32,1,256]{3,2,1,0:T(2,128)(2,1)S(1)}, bf16[1,32,1,256]{3,2,1,0:T(2,128)(2,1)S(1)}, u32[]{:S(2)}, u32[]{:S(2)}) collective-permute-start(bf16[1,32,1,256]{3,2,1,0:T(2,128)(2,1)S(1)} %get-tuple-element.31), channel_id=1, source_target_pairs={{0,4},{4,8},{8,12},{12,16},{16,20},{20,24},{24,28},{28,32},{32,36}... | collective-permute-start | bytes 49160 | tf_op jit(solution)/shard_map/ppermute | solution.py:19
  422.1 46.1 %collective-permute-start.5 = (bf16[1,32,1,256]{3,2,1,0:T(2,128)(2,1)S(1)}, bf16[1,32,1,256]{3,2,1,0:T(2,128)(2,1)S(1)}, u32[]{:S(2)}, u32[]{:S(2)}) collective-permute-start(bf16[1,32,1,256]{3,2,1,0:T(2,128)(2,1)S(1)} %get-tuple-element.32), channel_id=1, source_target_pairs={{4,0},{8,4},{12,8},{16,12},{20,16},{24,20},{28,24},{32,28},{36,32}... | collective-permute-start | bytes 49160 | tf_op jit(solution)/shard_map/ppermute | solution.py:21
  471.6 12.5 %collective-permute-start.6 = (bf16[1,32,66,1]{2,1,3,0:T(8,128)(2,1)S(1)}, bf16[1,32,66,1]{2,1,3,0:T(8,128)(2,1)S(1)}, u32[]{:S(2)}, u32[]{:S(2)}) collective-permute-start(bf16[1,32,66,1]{2,1,3,0:T(8,128)(2,1)S(1)} %copy.220), channel_id=1, source_target_pairs={{1,0},{2,1},{3,2},{5,4},{6,5},{7,6},{9,8},{10,9},{11,10},{13,12},{... | collective-permute-start | bytes 12680 | tf_op jit(solution)/shard_map/ppermute | solution.py:21
  474.3 11.0 %collective-permute-start.7 = (bf16[1,32,66,1]{2,1,3,0:T(8,128)(2,1)S(1)}, bf16[1,32,66,1]{2,1,3,0:T(8,128)(2,1)S(1)}, u32[]{:S(2)}, u32[]{:S(2)}) collective-permute-start(bf16[1,32,66,1]{2,1,3,0:T(8,128)(2,1)S(1)} %copy.228), channel_id=1, source_target_pairs={{0,1},{1,2},{2,3},{4,5},{5,6},{6,7},{8,9},{9,10},{10,11},{12,13},{... | collective-permute-start | bytes 12680 | tf_op jit(solution)/shard_map/ppermute | solution.py:19
  503.5 2.1 copy-start.11
  503.5 2.1 copy-start.10
Sparse Core Ops, SparseCore 0:
  13.3 102.5 reduce-scatter.2
  271.1 97.3 reduce-scatter.4
